TPU v7x, 128 devices: a whole 4x4x4 slice. The times are simulated.
128 devices in a mesh: group: 4 (over z_lo, core), dp: 2 (over z_hi), tensor: 16 (over x, y).
Axes of the slice: x: 4, y: 4, z: 4 (z_hi: 2, z_lo: 2; z = z_hi * 2 + z_lo), core: 2. Of those that a mesh axis runs over, the one named last changes fastest.
Arguments:
- tokens: bfloat16 [2048, 8, 2048], P('tensor', ('group', 'dp')), may hold values from -6 to 6
- cotangent: bfloat16 [2048, 8, 2048], P('tensor', ('group', 'dp')), may hold values from -6 to 6
- lengths: int32 [8], replicated, may hold values from 1 to 2048, 9830 in all
- ln1_gain: float32 [2048], replicated, may hold values from 0.25 to 1.75
- ln1_bias: float32 [2048], replicated, may hold values from -1.75 to 1.75
- w_qkv: bfloat16 [2048, 3, 16, 128], P(None, None, 'tensor'), may hold values from -0.125 to 0.125
- b_qv: float32 [2, 2048], P(None, 'tensor'), may hold values from -1.75 to 1.75
- w_o: bfloat16 [16, 128, 2048], P('tensor'), may hold values from -0.75 to 0.75
- b_o: float32 [2048], replicated, may hold values from -1.75 to 1.75
- ln2_gain: float32 [2048], replicated, may hold values from 0.25 to 1.75
- ln2_bias: float32 [2048], replicated, may hold values from -1.75 to 1.75
- w_in: bfloat16 [2048, 8192], P(None, 'tensor'), may hold values from -0.125 to 0.125
- b_in: float32 [8192], P('tensor'), may hold values from -1.75 to 1.75
- w_out: bfloat16 [8192, 2048], P('tensor'), may hold values from -0.0625 to 0.0625
- b_out: float32 [2048], replicated, may hold values from -1.75 to 1.75
Outputs:
- output: bfloat16 [2048, 8, 2048], P('tensor', ('group', 'dp'))
- input_grad: bfloat16 [2048, 8, 2048], P('tensor', ('group', 'dp'))
- d_ln1_gain: float32 [2048], P(('group', 'dp', 'tensor'))
- d_ln1_bias: float32 [2048], P(('group', 'dp', 'tensor'))
- d_w_qkv: float32 [2048, 3, 16, 128], P(('group', 'dp'), None, 'tensor')
- d_b_qv: float32 [2, 2048], P(None, ('group', 'dp', 'tensor'))
- d_w_o: float32 [16, 128, 2048], P('tensor', None, ('group', 'dp'))
- d_b_o: float32 [2048], P(('group', 'dp', 'tensor'))
- d_ln2_gain: float32 [2048], P(('group', 'dp', 'tensor'))
- d_ln2_bias: float32 [2048], P(('group', 'dp', 'tensor'))
- d_w_in: float32 [2048, 8192], P(('group', 'dp'), 'tensor')
- d_b_in: float32 [8192], P(('group', 'dp', 'tensor'))
- d_w_out: float32 [8192, 2048], P('tensor', ('group', 'dp'))
- d_b_out: float32 [2048], P(('group', 'dp', 'tensor'))
Inputs may be any that keep to these rules, and one draw needn't show every extreme that they name: The true lengths of the 8 sequences sum to 9830.
All inputs are finite; a program needn't handle non-finite values.
Results may differ from a plain program's by a relative error of at most 0.02.
Values may be sent and summed in bfloat16 or wider, within the bound.
No kernel may reach another device: no remote copies, remote signals or barrier semaphores. Data moves between devices by JAX's collectives and lax.ppermute only.
A program may use at most 192 MiB of HBM per device.

v0:
```python
from functools import partial
import math
import jax
import jax.numpy as jnp
from jax import lax
from jax.sharding import PartitionSpec as P

EPS = 1e-05
NEGATIVE = -1e30


def layer_norm(value, gain, shift):
    mean = jnp.mean(value, axis=-1, keepdims=True)
    centred = value - mean
    spread = jnp.mean(centred * centred, axis=-1, keepdims=True)
    return centred * lax.rsqrt(spread + EPS) * gain + shift


def gelu_tanh(value):
    return jax.nn.gelu(value, approximate=True)


def block_scores(rows_query, key_rows, first, length, score_scale):
    count = rows_query.shape[0]
    key_pos = jnp.arange(key_rows.shape[0], dtype=jnp.int32)
    query_pos = first + jnp.arange(count, dtype=jnp.int32)
    valid = (key_pos[None, :] <= query_pos[:, None]) & (key_pos[None, :] < length)
    scores = (
        lax.dot_general(
            rows_query, key_rows, (((1,), (1,)), ((), ())), preferred_element_type=jnp.float32
        )
        * score_scale
    )
    return (jnp.where(valid, scores, NEGATIVE), valid)


def attend_forward(item, block_rows, score_scale):
    query, key_rows, value_rows, length = item
    outputs = []
    log_parts = []
    for first in range(0, query.shape[0], block_rows):
        rows_query = query[first : first + block_rows]
        scores, valid = block_scores(rows_query, key_rows, first, length, score_scale)
        peak = jnp.max(scores, axis=-1, keepdims=True)
        expo = jnp.exp(scores - peak)
        weight_sum = jnp.sum(expo, axis=-1, keepdims=True)
        probs = (expo / weight_sum).astype(jnp.bfloat16)
        outputs.append(
            jnp.dot(probs, value_rows, preferred_element_type=jnp.float32).astype(jnp.bfloat16)
        )
        log_parts.append((peak + jnp.log(weight_sum))[:, 0])
    return (jnp.concatenate(outputs, 0), jnp.concatenate(log_parts, 0))


def attend_backward(item, block_rows, score_scale):
    query, key_rows, value_rows, length, grad_out, log_sums = item
    key_grad = jnp.zeros(key_rows.shape, jnp.float32)
    value_grad = jnp.zeros(value_rows.shape, jnp.float32)
    query_parts = []
    for first in range(0, query.shape[0], block_rows):
        rows_query = query[first : first + block_rows]
        scores, valid = block_scores(rows_query, key_rows, first, length, score_scale)
        probs = jnp.where(valid, jnp.exp(scores - log_sums[first : first + block_rows, None]), 0.0)
        grad_rows = grad_out[first : first + block_rows]
        probs_grad = lax.dot_general(
            grad_rows, value_rows, (((1,), (1,)), ((), ())), preferred_element_type=jnp.float32
        )
        inner = jnp.sum(probs * probs_grad, axis=-1, keepdims=True)
        score_grad = (probs * (probs_grad - inner)).astype(jnp.bfloat16)
        query_parts.append(
            jnp.dot(score_grad, key_rows, preferred_element_type=jnp.float32) * score_scale
        )
        key_grad = (
            key_grad
            + lax.dot_general(
                score_grad, rows_query, (((0,), (0,)), ((), ())), preferred_element_type=jnp.float32
            )
            * score_scale
        )
        value_grad = value_grad + lax.dot_general(
            probs.astype(jnp.bfloat16),
            grad_rows,
            (((0,), (0,)), ((), ())),
            preferred_element_type=jnp.float32,
        )
    return (
        jnp.concatenate(query_parts, 0).astype(jnp.bfloat16),
        key_grad.astype(jnp.bfloat16),
        value_grad.astype(jnp.bfloat16),
    )


def shards(
    tokens,
    cotangent,
    lengths,
    ln1_gain,
    ln1_bias,
    w_qkv,
    b_qv,
    w_o,
    b_o,
    ln2_gain,
    ln2_bias,
    w_in,
    b_in,
    w_out,
    b_out,
):
    row_count, seq_count, model_width = tokens.shape
    tensor_count = lax.axis_size("tensor")
    tensor_rank = lax.axis_index("tensor")
    seq_total = row_count * tensor_count
    local_heads = w_qkv.shape[2]
    head_size = w_qkv.shape[3]
    local_width = local_heads * head_size
    hidden = w_in.shape[1]
    block_rows = min(512, seq_total)
    score_scale = 1.0 / math.sqrt(head_size)
    group_count = lax.axis_size("group")
    group_rank = lax.axis_index("group")
    member = group_rank * lax.axis_size("dp") + lax.axis_index("dp")
    seq_lengths = lax.dynamic_slice_in_dim(lengths, member * seq_count, seq_count, 0)
    group_totals = jnp.sum(lengths.reshape(group_count, -1), axis=1).astype(jnp.float32)
    factor = (
        group_count
        * lax.dynamic_index_in_dim(group_totals, group_rank, 0, keepdims=False)
        / jnp.sum(group_totals)
    )
    inputs = tokens.astype(jnp.float32)
    normed_low = layer_norm(inputs, ln1_gain, ln1_bias).astype(jnp.bfloat16)
    normed_full = lax.all_gather(normed_low, "tensor", axis=0, tiled=True)
    joint_weight = w_qkv.reshape(model_width, 3 * local_width)
    projected = jnp.dot(
        normed_full.reshape(seq_total * seq_count, model_width),
        joint_weight,
        preferred_element_type=jnp.float32,
    )
    projected = projected.reshape(seq_total, seq_count, 3, local_width)
    query = (projected[:, :, 0] + b_qv[0]).astype(jnp.bfloat16)
    keys = projected[:, :, 1].astype(jnp.bfloat16)
    values = (projected[:, :, 2] + b_qv[1]).astype(jnp.bfloat16)

    def per_item(array):
        shaped = array.reshape(seq_total, seq_count, local_heads, head_size)
        return jnp.transpose(shaped, (1, 2, 0, 3)).reshape(
            seq_count * local_heads, seq_total, head_size
        )

    def per_row(array):
        shaped = array.reshape(seq_count, local_heads, seq_total, head_size)
        return jnp.transpose(shaped, (2, 0, 1, 3)).reshape(seq_total, seq_count, local_width)

    query_items = per_item(query)
    key_items = per_item(keys)
    value_items = per_item(values)
    item_lengths = jnp.repeat(seq_lengths, local_heads)
    heads_out, log_sums = lax.map(
        partial(attend_forward, block_rows=block_rows, score_scale=score_scale),
        (query_items, key_items, value_items, item_lengths),
    )
    attended = per_row(heads_out)
    out_weight = w_o.reshape(local_width, model_width)
    positions = tensor_rank * row_count + jnp.arange(row_count, dtype=jnp.int32)
    live = positions[:, None] < seq_lengths[None, :]
    upstream = jnp.where(live[:, :, None], cotangent, jnp.zeros_like(cotangent))
    upstream_full = lax.all_gather(upstream, "tensor", axis=0, tiled=True)
    attention_part = jnp.einsum(
        "rse,ed->rsd", attended, out_weight, preferred_element_type=jnp.float32
    ).astype(jnp.bfloat16)
    attention_part, upstream_full = lax.optimization_barrier((attention_part, upstream_full))
    attention = (
        lax.psum_scatter(attention_part, "tensor", scatter_dimension=0, tiled=True).astype(
            jnp.float32
        )
        + b_o
    )
    middle = inputs + attention
    second_low = layer_norm(middle, ln2_gain, ln2_bias).astype(jnp.bfloat16)
    second_full = lax.all_gather(second_low, "tensor", axis=0, tiled=True)
    pre_act = (
        jnp.dot(
            second_full.reshape(seq_total * seq_count, model_width),
            w_in,
            preferred_element_type=jnp.float32,
        )
        + b_in
    )
    activated = gelu_tanh(pre_act).astype(jnp.bfloat16).reshape(seq_total, seq_count, hidden)
    feed_part = jnp.einsum(
        "rsf,fd->rsd", activated, w_out, preferred_element_type=jnp.float32
    ).astype(jnp.bfloat16)
    piece = upstream_full
    weight_grad = jnp.einsum("rsf,rsd->fd", activated, piece, preferred_element_type=jnp.float32)
    part = jnp.einsum("rsd,fd->rsf", piece, w_out, preferred_element_type=jnp.float32)
    act_grad = part
    grad_w_out = weight_grad
    gelu_back = jax.vjp(gelu_tanh, pre_act)[1]
    pre_low = gelu_back(act_grad.reshape(seq_total * seq_count, hidden))[0].astype(jnp.bfloat16)
    grad_b_in = jnp.sum(pre_low, axis=0, dtype=jnp.float32)
    grad_w_in = jnp.einsum(
        "rd,rf->df",
        second_full.reshape(seq_total * seq_count, model_width),
        pre_low,
        preferred_element_type=jnp.float32,
    )
    pre_rows = pre_low.reshape(seq_total, seq_count, hidden)
    piece = pre_rows
    second_grad = lax.psum_scatter(
        jnp.einsum("rsf,df->rsd", piece, w_in, preferred_element_type=jnp.float32).astype(
            jnp.bfloat16
        ),
        "tensor",
        scatter_dimension=0,
        tiled=True,
    ).astype(jnp.float32)
    norm_two_back = jax.vjp(layer_norm, middle, ln2_gain, ln2_bias)[1]
    middle_part, grad_ln2_gain, grad_ln2_bias = norm_two_back(second_grad)
    middle_grad = upstream.astype(jnp.float32) + middle_part
    branch_low = middle_grad.astype(jnp.bfloat16)
    grad_b_o = jnp.sum(branch_low, axis=(0, 1), dtype=jnp.float32)
    grad_b_out = jnp.sum(upstream, axis=(0, 1), dtype=jnp.float32)
    piece = lax.all_gather(branch_low, "tensor", axis=0, tiled=True)
    feed_part, piece = lax.optimization_barrier((feed_part, piece))
    feed = (
        lax.psum_scatter(feed_part, "tensor", scatter_dimension=0, tiled=True).astype(jnp.float32)
        + b_out
    )
    output = (middle + feed).astype(jnp.bfloat16)
    weight_grad = jnp.einsum("rse,rsd->ed", attended, piece, preferred_element_type=jnp.float32)
    part = jnp.einsum("rsd,ed->rse", piece, out_weight, preferred_element_type=jnp.float32)
    head_items = per_item(part.astype(jnp.bfloat16))
    grads_query, grads_keys, grads_values = lax.map(
        partial(attend_backward, block_rows=block_rows, score_scale=score_scale),
        (query_items, key_items, value_items, item_lengths, head_items, log_sums),
    )
    joint_grad = jnp.stack(
        (per_row(grads_query), per_row(grads_keys), per_row(grads_values)), axis=2
    )
    grad_b_qv = jnp.sum(joint_grad[:, :, 0::2], axis=(0, 1), dtype=jnp.float32)
    joint_rows = joint_grad.reshape(seq_total, seq_count, 3 * local_width)
    grad_w_qkv = jnp.einsum(
        "rd,rc->dc",
        normed_full.reshape(seq_total * seq_count, model_width),
        joint_rows.reshape(seq_total * seq_count, 3 * local_width),
        preferred_element_type=jnp.float32,
    )
    piece = joint_rows
    normed_grad = lax.psum_scatter(
        jnp.einsum("rsc,dc->rsd", piece, joint_weight, preferred_element_type=jnp.float32).astype(
            jnp.bfloat16
        ),
        "tensor",
        scatter_dimension=0,
        tiled=True,
    ).astype(jnp.float32)
    norm_one_back = jax.vjp(layer_norm, inputs, ln1_gain, ln1_bias)[1]
    input_part, grad_ln1_gain, grad_ln1_bias = norm_one_back(normed_grad)
    input_grad = (middle_grad + input_part).astype(jnp.bfloat16)
    summed = (
        halving_sum(grad_w_qkv.reshape(model_width, 3, local_heads, head_size) * factor, 0),
        halving_sum(weight_grad.reshape(local_heads, head_size, model_width) * factor, 2),
        halving_sum(grad_w_in * factor, 0),
        halving_sum(grad_w_out * factor, 1),
    )
    in_full = lax.dynamic_update_slice_in_dim(
        jnp.zeros((hidden * tensor_count,), jnp.float32), grad_b_in, tensor_rank * hidden, 0
    )
    joint_full = lax.dynamic_update_slice_in_dim(
        jnp.zeros((2, local_width * tensor_count), jnp.float32),
        grad_b_qv,
        tensor_rank * local_width,
        1,
    )
    shard_count = group_count * lax.axis_size("dp")
    vectors = (
        grad_ln1_gain,
        grad_ln1_bias,
        grad_b_o,
        grad_ln2_gain,
        grad_ln2_bias,
        grad_b_out,
        joint_full[0],
        joint_full[1],
        in_full,
    )
    pieces = [
        jnp.transpose((item * factor).reshape(shard_count, tensor_count, -1), (1, 0, 2))
        for item in vectors
    ]
    widths = [piece.shape[2] for piece in pieces]
    packed = jnp.concatenate(pieces, 2)
    packed = halving_steps(
        packed,
        0,
        [
            ("tensor", tensor_count, 8),
            ("tensor", tensor_count, 4),
            ("tensor", tensor_count, 2),
            ("tensor", tensor_count, 1),
        ],
    )
    packed = halving_steps(
        packed,
        1,
        [("group", group_count, 2), ("group", group_count, 1), ("dp", lax.axis_size("dp"), 1)],
    )
    flat = packed.reshape(-1)
    parts = []
    offset = 0
    for width in widths:
        parts.append(flat[offset : offset + width])
        offset += width
    return (
        output,
        input_grad,
        parts[0],
        parts[1],
        summed[0],
        jnp.stack((parts[6], parts[7])),
        summed[1],
        parts[2],
        parts[3],
        parts[4],
        summed[2],
        parts[8],
        summed[3],
        parts[5],
    )


def halving_steps(value, dim, steps, send_type=None):
    for axis, size, bit in steps:
        half = value.shape[dim] // 2
        low_half = lax.slice_in_dim(value, 0, half, axis=dim)
        high_half = lax.slice_in_dim(value, half, 2 * half, axis=dim)
        upper = lax.axis_index(axis) // bit % 2 == 1
        keep = jnp.where(upper, high_half, low_half)
        send = jnp.where(upper, low_half, high_half)
        if send_type is not None:
            send = send.astype(send_type)
        got = lax.ppermute(send, axis, [(i, i ^ bit) for i in range(size)])
        value = keep + got.astype(keep.dtype)
    return value


def halving_sum(value, dim):
    shape = value.shape
    groups = lax.axis_size("group")
    dps = lax.axis_size("dp")
    split = shape[:dim] + (groups * dps, shape[dim] // (groups * dps)) + shape[dim + 1 :]
    value = value.reshape(split)
    value = halving_steps(
        value, dim, [("group", groups, 2), ("group", groups, 1), ("dp", dps, 1)], jnp.bfloat16
    )
    return value.reshape(shape[:dim] + (shape[dim] // (groups * dps),) + shape[dim + 1 :])


def solution(mesh):
    in_specs = (
        P("tensor", ("group", "dp"), None),
        P("tensor", ("group", "dp"), None),
        P(),
        P(),
        P(),
        P(None, None, "tensor", None),
        P(None, "tensor"),
        P("tensor", None, None),
        P(),
        P(),
        P(),
        P(None, "tensor"),
        P("tensor"),
        P("tensor", None),
        P(),
    )
    out_specs = (
        P("tensor", ("group", "dp"), None),
        P("tensor", ("group", "dp"), None),
        P(("group", "dp", "tensor")),
        P(("group", "dp", "tensor")),
        P(("group", "dp"), None, "tensor", None),
        P(None, ("group", "dp", "tensor")),
        P("tensor", None, ("group", "dp")),
        P(("group", "dp", "tensor")),
        P(("group", "dp", "tensor")),
        P(("group", "dp", "tensor")),
        P(("group", "dp"), "tensor"),
        P(("group", "dp", "tensor")),
        P("tensor", ("group", "dp")),
        P(("group", "dp", "tensor")),
    )
    return jax.shard_map(shards, mesh=mesh, in_specs=in_specs, out_specs=out_specs, check_vma=False)
```

profile of v0, /device:TPU:0, one launch (start us, length us, event | category | flops | bytes accessed | tf_op | source)
XLA Modules:
  0.0 779.4 jit_solution(8731599573753859071)
XLA Ops:
  20.3 65.2 %all-gather.5.cloned.1.call-done = bf16[2048,1,2048]{2,0,1:T(8,128)(2,1)} async-done(((bf16[128,1,2048]{2,0,1:T(8,128)(2,1)}), bf16[2048,1,2048]{2,0,1:T(8,128)(2,1)}) %all-gather.5.cloned.1.call-update) | async-done | bytes 8388624 | tf_op jit(solution)/shard_map/all_gather | solution.py:132
  85.5 7.4 fusion.33
  98.0 4.2 online-softmax.3
  103.2 5.2 fusion.126
  113.4 5.2 fusion.125
  123.6 4.8 fusion.124
  128.4 4.4 online-softmax
  133.8 5.6 convert_bitcast_fusion.3
  139.4 19.1 %all-gather.7.cloned.1.call-done = bf16[2048,1,2048]{2,0,1:T(8,128)(2,1)} async-done(((bf16[128,1,2048]{2,0,1:T(8,128)(2,1)}), bf16[2048,1,2048]{2,0,1:T(8,128)(2,1)}) %all-gather.7.cloned.1.call-update) | async-done | bytes 8388624 | tf_op jit(solution)/shard_map/all_gather | solution.py:167
  158.6 88.1 %reduce-scatter.5.cloned.1.call-done = bf16[128,1,2048]{2,0,1:T(8,128)(2,1)} async-done(((bf16[2048,1,2048]{2,0,1:T(8,128)(2,1)}), bf16[128,1,2048]{2,0,1:T(8,128)(2,1)}) %reduce-scatter.5.cloned.1.call-update) | async-done | bytes 524304 | tf_op jit(solution)/shard_map/reduce_scatter | solution.py:173
  251.7 70.2 %all-gather.9.cloned.1.call-done = bf16[2048,1,2048]{2,0,1:T(8,128)(2,1)} async-done(((bf16[128,1,2048]{2,0,1:T(8,128)(2,1)}), bf16[2048,1,2048]{2,0,1:T(8,128)(2,1)}) %all-gather.9.cloned.1.call-update) | async-done | bytes 8388624 | tf_op jit(solution)/shard_map/all_gather | solution.py:180
  321.9 7.5 fusion.10
  329.4 13.1 %convert_reduce_fusion = (f32[512]{0:T(512)}, bf16[2048,512]{1,0:T(8,128)(2,1)S(1)}) fusion(f32[2048,512]{1,0:T(8,128)S(1)} %fusion.10, f32[512]{0:T(512)S(1)} %copy-done.85, bf16[512,2048]{1,0:T(8,128)(2,1)S(1)} %copy-done, bf16[2048,1,2048]{2,0,1:T(8,128)(2,1)} %all-gather.7.cloned.1.call-done), kind=kOutput, calls=%fused_computation.29 | convolution fusion | flops 4319084032 | bytes 16781312 | tf_op jit(solution)/shard_map/rsd,fd->rsf/dot_general | solution.py:195
  343.9 6.9 convert_bitcast_fusion.1
  350.9 84.8 %reduce-scatter.7.cloned.1.call-done = bf16[128,1,2048]{2,0,1:T(8,128)(2,1)} async-done(((bf16[2048,1,2048]{2,0,1:T(8,128)(2,1)}), bf16[128,1,2048]{2,0,1:T(8,128)(2,1)}) %reduce-scatter.7.cloned.1.call-update) | async-done | bytes 524304 | tf_op jit(solution)/shard_map/reduce_scatter | solution.py:209
  450.4 15.8 %convert_bitcast_fusion.2 = bf16[2048,1,2048]{2,0,1:T(8,128)(2,1)} fusion(bf16[512,2048]{1,0:T(8,128)(2,1)S(1)} %copy-done, f32[2048,512]{1,0:T(8,128)S(1)} %copy-done.89, f32[512]{0:T(512)S(1)} %copy-done.85), kind=kOutput, calls=%fused_computation.18 | convolution fusion | flops 4309647360 | bytes 14682112 | tf_op jit(solution)/shard_map/rsf,fd->rsd/dot_general | solution.py:190
  466.2 45.6 %all-gather.11.cloned.1.call-done = bf16[2048,1,2048]{2,0,1:T(8,128)(2,1)} async-done(((bf16[128,1,2048]{2,0,1:T(8,128)(2,1)}), bf16[2048,1,2048]{2,0,1:T(8,128)(2,1)}) %all-gather.11.cloned.1.call-update) | async-done | bytes 8388624 | tf_op jit(solution)/shard_map/all_gather | solution.py:223
  511.8 5.8 fusion.45
  530.8 10.9 %multiply_reduce_fusion = (f32[512]{0:T(512)}, f32[512]{0:T(512)}, f32[512]{0:T(512)}, f32[512]{0:T(512)}, f32[512,2048]{1,0:T(8,128)}) fusion(f32[512,2048]{1,0:T(8,128)S(1)} %copy-done.2, f32[512]{0:T(512)S(1)} %copy-done.59, pred[2048]{0:T(1024)(128)(4,1)S(1)} %iota_compare_fusion.4, s32[512]{0:T(512)S(1)} %copy-done.52, f32[512,2048]{1,0:T(8,128)} %fusion.108, ...), kind=kOutput, calls=%fused_computation.31 | convolution fusion | flops 293599232 | bytes 34234368 | tf_op jit(solution)/shard_map/while/body/eval_jaxpr/dot_general | solution.py:65
  541.7 9.5 %multiply_convert_fusion = (bf16[512,2048]{1,0:T(8,128)(2,1)S(1)}, bf16[512,2048]{1,0:T(8,128)(2,1)}, bf16[512,2048]{1,0:T(8,128)(2,1)S(1)}) fusion(f32[512,2048]{1,0:T(8,128)} %get-tuple-element.119, f32[512]{0:T(512)} %get-tuple-element.82, f32[512,2048]{1,0:T(8,128)S(1)} %copy-done.2, f32[512]{0:T(512)} %get-tuple-element.124, ...), kind=kLoop, calls=%fused_computation.30 | loop fusion | flops 22020096 | bytes 31475712 | tf_op jit(solution)/shard_map/while/body/eval_jaxpr/convert_element_type | solution.py:69
  569.4 9.7 %convert_bitcast_fusion = bf16[2048,1,2048]{2,0,1:T(8,128)(2,1)} fusion(bf16[2048,384]{0,1:T(8,128)(2,1)} %bitcast.201, bf16[2048,384]{0,1:T(8,128)(2,1)} %bitcast.202), kind=kOutput, calls=%fused_computation.16 | convolution fusion | flops 3225419776 | bytes 11534336 | tf_op jit(solution)/shard_map/rsc,dc->rsd/dot_general | solution.py:250
  582.5 8.5 %fusion.27 = f32[512,2048]{1,0:T(8,128)S(1)} fusion(bf16[2048,1,2048]{2,0,1:T(8,128)(2,1)} %all-gather.7.cloned.1.call-done, f32[]{:T(128)S(6)} %div.167, f32[2048,512]{1,0:T(8,128)} %copy-done.88, f32[512]{0:T(512)S(1)} %copy-done.86), kind=kOutput, calls=%fused_computation.59 | convolution fusion | flops 4306501632 | bytes 16779268 | tf_op jit(solution)/shard_map/rsf,rsd->fd/dot_general | solution.py:194
  596.6 7.1 fusion.30
  614.4 17.2 %collective-permute-done.13 = bf16[4,256,512]{2,1,0:T(8,128)(2,1)} collective-permute-done((bf16[4,256,512]{2,1,0:T(8,128)(2,1)}, bf16[4,256,512]{2,1,0:T(8,128)(2,1)}, u32[]{:S(2)}, u32[]{:S(2)}) %collective-permute-start.13) | collective-permute-done | bytes 1048608 | tf_op jit(solution)/shard_map/ppermute | solution.py:342
  633.4 19.6 %collective-permute-done.16 = bf16[512,4,256]{2,0,1:T(8,128)(2,1)} collective-permute-done((bf16[512,4,256]{2,0,1:T(8,128)(2,1)}, bf16[512,4,256]{2,0,1:T(8,128)(2,1)}, u32[]{:S(2)}, u32[]{:S(2)}) %collective-permute-start.16) | collective-permute-done | bytes 1048608 | tf_op jit(solution)/shard_map/ppermute | solution.py:342
  661.9 5.2 collective-permute-done.15
  668.0 4.4 collective-permute-done.18
  676.4 4.7 fusion.42
  683.5 7.0 fusion.36
  709.7 26.8 %collective-permute-done.7 = bf16[4,256,3,1,128]{4,3,2,1,0:T(2,128)(2,1)} collective-permute-done((bf16[4,256,3,1,128]{4,3,2,1,0:T(2,128)(2,1)S(1)}, bf16[4,256,3,1,128]{4,3,2,1,0:T(2,128)(2,1)}, u32[]{:S(2)}, u32[]{:S(2)}) %collective-permute-start.7) | collective-permute-done | bytes 786464 | tf_op jit(solution)/shard_map/ppermute | solution.py:342
  736.5 4.7 copy_add_fusion
  755.1 7.4 collective-permute-done.9
  (371 shorter events, 160.5 us)
Async XLA Ops:
  7.2 322.2 %copy-start = (bf16[512,2048]{1,0:T(8,128)(2,1)S(1)}, bf16[512,2048]{1,0:T(8,128)(2,1)}, u32[]{:S(2)}) copy-start(bf16[512,2048]{1,0:T(8,128)(2,1)} %param.28) | copy-start | bytes 6291460
  7.2 78.3 %all-gather.5.cloned.1.call-start = ((), (), s32[]{:S(2)}) async-start(), calls=%async_computation.4 | async-start | bytes 8912896 | tf_op jit(solution)/shard_map/all_gather | solution.py:132
  12.2 146.3 %all-gather.7.cloned.1.call-start = ((), (), s32[]{:S(2)}) async-start(), calls=%async_computation.5 | async-start | bytes 8912896 | tf_op jit(solution)/shard_map/all_gather | solution.py:167
  16.8 229.8 %reduce-scatter.5.cloned.1.call-start = ((), (), s32[]{:S(2)}) async-start(), calls=%async_computation.6 | async-start | bytes 8912896 | tf_op jit(solution)/shard_map/reduce_scatter | solution.py:173
  139.4 107.3 %copy-start.9 = (bf16[128,1,2048]{2,0,1:T(8,128)(2,1)S(1)}, bf16[128,1,2048]{2,0,1:T(8,128)(2,1)}, u32[]{:S(2)}) copy-start(bf16[128,1,2048]{2,0,1:T(8,128)(2,1)} %param.15) | copy-start | bytes 1572868
  139.4 107.3 %copy-start.39 = (f32[2048]{0:T(1024)S(1)}, f32[2048]{0:T(1024)}, u32[]{:S(2)}) copy-start(f32[2048]{0:T(1024)} %param.23) | copy-start | bytes 24580
  139.4 110.0 %copy-start.47 = (f32[2048]{0:T(1024)S(1)}, f32[2048]{0:T(1024)}, u32[]{:S(2)}) copy-start(f32[2048]{0:T(1024)} %param.24) | copy-start | bytes 24580
  139.4 110.0 %copy-start.70 = (f32[2048]{0:T(1024)S(1)}, f32[2048]{0:T(1024)}, u32[]{:S(2)}) copy-start(f32[2048]{0:T(1024)} %param.25) | copy-start | bytes 24580
  158.6 163.3 %all-gather.9.cloned.1.call-start = ((), (), s32[]{:S(2)}) async-start(), calls=%async_computation.7 | async-start | bytes 8912896 | tf_op jit(solution)/shard_map/all_gather | solution.py:180
  251.6 184.1 %reduce-scatter.7.cloned.1.call-start = ((), (), s32[]{:S(2)}) async-start(), calls=%async_computation.8 | async-start | bytes 8912896 | tf_op jit(solution)/shard_map/reduce_scatter | solution.py:209
  350.9 160.9 %all-gather.11.cloned.1.call-start = ((), (), s32[]{:S(2)}) async-start(), calls=%async_computation.9 | async-start | bytes 8912896 | tf_op jit(solution)/shard_map/all_gather | solution.py:223
  441.6 260.6 %reduce-scatter.11.cloned.1.call-start = ((), (), s32[]{:S(2)}) async-start(), calls=%async_computation.11 | async-start | bytes 8912896 | tf_op jit(solution)/shard_map/reduce_scatter | solution.py:249
  579.1 186.7 %reduce-scatter.9.cloned.1.call-start = ((), (), s32[]{:S(2)}) async-start(), calls=%async_computation.10 | async-start | bytes 8912896 | tf_op jit(solution)/shard_map/reduce_scatter | solution.py:226
  605.1 26.5 %collective-permute-start.13 = (bf16[4,256,512]{2,1,0:T(8,128)(2,1)}, bf16[4,256,512]{2,1,0:T(8,128)(2,1)}, u32[]{:S(2)}, u32[]{:S(2)}) collective-permute-start(bf16[4,256,512]{2,1,0:T(8,128)(2,1)} %bitcast.57), channel_id=1, source_target_pairs={{0,64},{32,96},{64,0},{96,32},{1,65},{33,97},{65,1},{97,33},{2,66}... | collective-permute-start | bytes 3145736 | tf_op jit(solution)/shard_map/ppermute | solution.py:342
  610.4 42.5 %collective-permute-start.16 = (bf16[512,4,256]{2,0,1:T(8,128)(2,1)}, bf16[512,4,256]{2,0,1:T(8,128)(2,1)}, u32[]{:S(2)}, u32[]{:S(2)}) collective-permute-start(bf16[512,4,256]{2,0,1:T(8,128)(2,1)} %select_convert_fusion), channel_id=1, source_target_pairs={{0,64},{32,96},{64,0},{96,32},{1,65},{33,97},{65,1},{97,33},{2,66}... | collective-permute-start | bytes 3145736 | tf_op jit(solution)/shard_map/ppermute | solution.py:342
  633.3 21.9 %collective-permute-start.14 = (bf16[2,256,512]{2,1,0:T(8,128)(2,1)S(1)}, bf16[2,256,512]{2,1,0:T(8,128)(2,1)S(1)}, u32[]{:S(2)}, u32[]{:S(2)}) collective-permute-start(bf16[2,256,512]{2,1,0:T(8,128)(2,1)S(1)} %select_convert_fusion.4), channel_id=1, source_target_pairs={{0,32},{32,0},{64,96},{96,64},{1,33},{33,1},{65,97},{97,65},{2,34}... | collective-permute-start | bytes 1572872 | tf_op jit(solution)/shard_map/ppermute | solution.py:342
  655.0 4.4 collective-permute-start.17
  656.2 10.9 %collective-permute-start.15 = (bf16[1,256,512]{2,1,0:T(8,128)(2,1)}, bf16[1,256,512]{2,1,0:T(8,128)(2,1)S(1)}, u32[]{:S(2)}, u32[]{:S(2)}) collective-permute-start(bf16[1,256,512]{2,1,0:T(8,128)(2,1)} %select_convert_fusion.6), channel_id=1, source_target_pairs={{0,16},{16,0},{1,17},{17,1},{2,18},{18,2},{3,19},{19,3},{4,20},{20... | collective-permute-start | bytes 786440 | tf_op jit(solution)/shard_map/ppermute | solution.py:342
  660.4 12.0 %collective-permute-start.18 = (bf16[512,1,256]{2,0,1:T(8,128)(2,1)}, bf16[512,1,256]{2,0,1:T(8,128)(2,1)}, u32[]{:S(2)}, u32[]{:S(2)}) collective-permute-start(bf16[512,1,256]{2,0,1:T(8,128)(2,1)} %select_convert_fusion.5), channel_id=1, source_target_pairs={{0,16},{16,0},{1,17},{17,1},{2,18},{18,2},{3,19},{19,3},{4,20},{20... | collective-permute-start | bytes 786440 | tf_op jit(solution)/shard_map/ppermute | solution.py:342
  681.8 10.1 %collective-permute-start.10 = (bf16[1,128,4,256]{3,1,2,0:T(8,128)(2,1)S(1)}, bf16[1,128,4,256]{3,1,2,0:T(8,128)(2,1)S(1)}, u32[]{:S(2)}, u32[]{:S(2)}) collective-permute-start(bf16[1,128,4,256]{3,1,2,0:T(8,128)(2,1)S(1)} %select_convert_fusion.7), channel_id=1, source_target_pairs={{0,64},{32,96},{64,0},{96,32},{1,65},{33,97},{65,1},{97,33},{2,66}... | collective-permute-start | bytes 786440 | tf_op jit(solution)/shard_map/ppermute | solution.py:342
  692.2 1.4 collective-permute-start.11
  694.4 6.3 collective-permute-start.12
  700.2 36.4 %collective-permute-start.7 = (bf16[4,256,3,1,128]{4,3,2,1,0:T(2,128)(2,1)S(1)}, bf16[4,256,3,1,128]{4,3,2,1,0:T(2,128)(2,1)}, u32[]{:S(2)}, u32[]{:S(2)}) collective-permute-start(bf16[4,256,3,1,128]{4,3,2,1,0:T(2,128)(2,1)S(1)} %copy.55), channel_id=1, source_target_pairs={{0,64},{32,96},{64,0},{96,32},{1,65},{33,97},{65,1},{97,33},{2,66}... | collective-permute-start | bytes 2359304 | tf_op jit(solution)/shard_map/ppermute | solution.py:342
  706.6 34.6 %collective-permute-start = (f32[8,8,192]{2,0,1:T(8,128)S(1)}, f32[8,8,192]{2,0,1:T(8,128)S(1)}, u32[]{:S(2)}, u32[]{:S(2)}) collective-permute-start(f32[8,8,192]{2,0,1:T(8,128)S(1)} %slice_select_fusion.2), channel_id=1, source_target_pairs={{0,8},{1,9},{2,10},{3,11},{4,12},{5,13},{6,14},{7,15},{8,0},{9,1},... | collective-permute-start | bytes 147464 | tf_op jit(solution)/shard_map/ppermute | solution.py:342
  741.3 4.5 collective-permute-start.1
  743.6 5.4 collective-permute-start.8
  745.9 5.4 collective-permute-start.2
  751.3 3.7 collective-permute-start.3
  753.2 9.4 %collective-permute-start.9 = (bf16[1,256,3,1,128]{4,3,2,1,0:T(2,128)(2,1)S(1)}, bf16[1,256,3,1,128]{4,3,2,1,0:T(2,128)(2,1)S(1)}, u32[]{:S(2)}, u32[]{:S(2)}) collective-permute-start(bf16[1,256,3,1,128]{4,3,2,1,0:T(2,128)(2,1)S(1)} %fusion.96), channel_id=1, source_target_pairs={{0,16},{16,0},{1,17},{17,1},{2,18},{18,2},{3,19},{19,3},{4,20},{20... | collective-permute-start | bytes 589832 | tf_op jit(solution)/shard_map/ppermute | solution.py:342
  755.1 9.0 %collective-permute-start.4 = (f32[1,4,192]{2,0,1:T(1,128)S(1)}, f32[1,4,192]{2,0,1:T(1,128)S(1)}, u32[]{:S(2)}, u32[]{:S(2)}) collective-permute-start(f32[1,4,192]{2,0,1:T(1,128)S(1)} %broadcast_select_fusion.8), channel_id=1, source_target_pairs={{0,64},{32,96},{64,0},{96,32},{1,65},{33,97},{65,1},{97,33},{2,66}... | collective-permute-start | bytes 9224 | tf_op jit(solution)/shard_map/ppermute | solution.py:342
  764.0 1.2 collective-permute-start.5
  765.3 5.2 collective-permute-start.6
  (87 other events, 1435.8 us)
Sparse Core Ops, SparseCore 0:
  12.4 73.0 all-gather.4
  88.2 70.3 all-gather.6
  162.0 84.6 reduce-scatter.4
  251.8 70.0 all-gather.8
  351.0 84.6 reduce-scatter.6
  441.7 70.0 all-gather.10
  579.2 84.8 reduce-scatter.10
  667.6 85.7 reduce-scatter.8
where the time goes:
time: 789 us; the launch traced here: 779 us
  waiting for transfers between devices  461 us (58%)
  matrix products  155 us (20%)
  other arithmetic  78.1 us (10%)
  local copies, waits for them, and re-layouts  28.2 us (4%)
  starting transfers between devices  22.8 us (3%)
  between operations  17.3 us (2%)
  Pallas kernels  16.6 us (2%)
    ppermute x19, waiting for transfers between devices, halving_steps(): got = lax.ppermute(send, axis, [(i, i ^ bit) for i in range(size)])  88.2 us
    reduce_scatter x1, waiting for transfers between devices, shards(): lax.psum_scatter(attention_part, 'tensor', scatter_dimension=0, tiled=True)  88.1 us
    reduce_scatter x1, waiting for transfers between devices, shards(): lax.psum_scatter(jnp.einsum('rsf,df->rsd', piece, w_in, preferred_element...  84.8 us
    all_gather x1, waiting for transfers between devices, shards(): second_full = lax.all_gather(second_low, 'tensor', axis=0, tiled=True)  70.2 us
    all_gather x1, waiting for transfers between devices, shards(): normed_full = lax.all_gather(normed_low, 'tensor', axis=0, tiled=True)  65.2 us
    all_gather x1, waiting for transfers between devices, shards(): piece = lax.all_gather(branch_low, 'tensor', axis=0, tiled=True)  45.6 us
    ppermute x19, starting transfers between devices, halving_steps(): got = lax.ppermute(send, axis, [(i, i ^ bit) for i in range(size)])  22.5 us
    dot_general x4, matrix products, attend_backward(): lax.dot_general(grad_rows, value_rows, (((1,), (1,)), ((), ())), preferre...  21.5 us
  transfers between devices with their start and end apart: 27, of which 19 were waited for; matrix products, arithmetic and copies ran while one was open for 18% of the time, Pallas kernels for 2%

commit v1 on v0

--- a/solution.py
+++ b/solution.py
@@ -7,6 +7,28 @@
 
 EPS = 1e-05
 NEGATIVE = -1e30
+
+
+def in_order(blocks, dim):
+    lengths = list(blocks.shape[1:])
+    lengths[dim] *= blocks.shape[0]
+    return jnp.moveaxis(blocks, 0, dim).reshape(lengths)
+
+
+def ring_gather(value, axis, dim):
+    size = lax.axis_size(axis)
+    pairs = [(i, (i + 1) % size) for i in range(size)]
+    back = [(b, a) for a, b in pairs]
+    lower, upper = ([], [])
+    for step in range(size - 1):
+        if step % 2 == 0:
+            lower.append(lax.ppermute(lower[-1] if lower else value, axis, pairs))
+        else:
+            upper.append(lax.ppermute(upper[-1] if upper else value, axis, back))
+    tiles = jnp.stack([*lower[::-1], value, *upper])
+    shift = lax.axis_index(axis) - len(lower)
+    tiles = tiles[(jnp.arange(size) - shift) % size]
+    return in_order(tiles, dim)
 
 
 def layer_norm(value, gain, shift):
@@ -220,7 +242,7 @@
     branch_low = middle_grad.astype(jnp.bfloat16)
     grad_b_o = jnp.sum(branch_low, axis=(0, 1), dtype=jnp.float32)
     grad_b_out = jnp.sum(upstream, axis=(0, 1), dtype=jnp.float32)
-    piece = lax.all_gather(branch_low, "tensor", axis=0, tiled=True)
+    piece = ring_gather(branch_low, "tensor", 0)
     feed_part, piece = lax.optimization_barrier((feed_part, piece))
     feed = (
         lax.psum_scatter(feed_part, "tensor", scatter_dimension=0, tiled=True).astype(jnp.float32)

time: 789 us -> 843 us (1.068)
  local copies, waits for them, and re-layouts: 28.2 us -> 64.3 us
  starting transfers between devices: 22.8 us -> 55.8 us
  matrix products: 155 us -> 142 us
    ppermute x0 -> x15, waiting for transfers between devices: none -> 55.2 us  [the longest x8 53.4 us: ring_gather(): lower.append(lax.ppermute(lower[-1] if lower else value, axis, pairs))]
    all_gather x1 -> x0, waiting for transfers between devices: 45.6 us -> none  [shards(): piece = lax.all_gather(branch_low, 'tensor', axis=0, tiled=True)]
    ppermute x0 -> x15, starting transfers between devices: none -> 40.2 us  [the longest x7 38.8 us: ring_gather(): upper.append(lax.ppermute(upper[-1] if upper else value, axis, back))]
    unnamed x187 -> x226, local copies, waits for them, and re-layouts: 15.3 us -> 38.6 us
    ppermute x19, waiting for transfers between devices: 88.2 us -> 75.6 us  [halving_steps(): got = lax.ppermute(send, axis, [(i, i ^ bit) for i in range(size)])]
    dot_general x1, matrix products: 15.8 us -> 7.23 us  [shards(): jnp.einsum('rsf,fd->rsd', activated, w_out, preferred_element_type=jnp.fl...]
  transfers between devices with their start and end apart: 27 -> 41, of which waited for: 19 -> 27; matrix products, arithmetic and copies ran while one was open for 18% -> 20% of each run, Pallas kernels for 2% -> 2%
where the time goes in v1:
time: 843 us; the launch traced here: 833 us
  waiting for transfers between devices  458 us (54%)
  matrix products  142 us (17%)
  other arithmetic  78.7 us (9%)
  local copies, waits for them, and re-layouts  64.3 us (8%)
  starting transfers between devices  55.8 us (7%)
  between operations  17.5 us (2%)
  Pallas kernels  16.5 us (2%)
    reduce_scatter x1, waiting for transfers between devices, shards(): lax.psum_scatter(attention_part, 'tensor', scatter_dimension=0, tiled=True)  88.1 us
    reduce_scatter x1, waiting for transfers between devices, shards(): lax.psum_scatter(jnp.einsum('rsf,df->rsd', piece, w_in, preferred_element...  84.2 us
    ppermute x19, waiting for transfers between devices, halving_steps(): got = lax.ppermute(send, axis, [(i, i ^ bit) for i in range(size)])  75.6 us
    all_gather x1, waiting for transfers between devices, shards(): second_full = lax.all_gather(second_low, 'tensor', axis=0, tiled=True)  70.2 us
    all_gather x1, waiting for transfers between devices, shards(): normed_full = lax.all_gather(normed_low, 'tensor', axis=0, tiled=True)  65.2 us
    ppermute x8, waiting for transfers between devices, ring_gather(): lower.append(lax.ppermute(lower[-1] if lower else value, axis, pairs))  53.4 us
    ppermute x7, starting transfers between devices, ring_gather(): upper.append(lax.ppermute(upper[-1] if upper else value, axis, back))  38.8 us
    unnamed x226, local copies, waits for them, and re-layouts  38.6 us
  transfers between devices with their start and end apart: 41, of which 27 were waited for; matrix products, arithmetic and copies ran while one was open for 20% of the time, Pallas kernels for 2%

profile of v1, /device:TPU:0, one launch (start us, length us, event | category | flops | bytes accessed | tf_op | source)
XLA Modules:
  0.0 832.6 jit_solution(3685792049873574825)
XLA Ops:
  20.3 65.2 %all-gather.4.cloned.1.call-done = bf16[2048,1,2048]{2,0,1:T(8,128)(2,1)} async-done(((bf16[128,1,2048]{2,0,1:T(8,128)(2,1)}), bf16[2048,1,2048]{2,0,1:T(8,128)(2,1)}) %all-gather.4.cloned.1.call-update) | async-done | bytes 8388624 | tf_op jit(solution)/shard_map/all_gather | solution.py:154
  85.5 7.4 fusion.33
  133.8 5.6 convert_bitcast_fusion.3
  139.5 19.1 %all-gather.6.cloned.1.call-done = bf16[2048,1,2048]{2,0,1:T(8,128)(2,1)} async-done(((bf16[128,1,2048]{2,0,1:T(8,128)(2,1)}), bf16[2048,1,2048]{2,0,1:T(8,128)(2,1)}) %all-gather.6.cloned.1.call-update) | async-done | bytes 8388624 | tf_op jit(solution)/shard_map/all_gather | solution.py:189
  158.6 88.1 %reduce-scatter.5.cloned.1.call-done = bf16[128,1,2048]{2,0,1:T(8,128)(2,1)} async-done(((bf16[2048,1,2048]{2,0,1:T(8,128)(2,1)}), bf16[128,1,2048]{2,0,1:T(8,128)(2,1)}) %reduce-scatter.5.cloned.1.call-update) | async-done | bytes 524304 | tf_op jit(solution)/shard_map/reduce_scatter | solution.py:195
  251.7 70.2 %all-gather.8.cloned.1.call-done = bf16[2048,1,2048]{2,0,1:T(8,128)(2,1)} async-done(((bf16[128,1,2048]{2,0,1:T(8,128)(2,1)}), bf16[2048,1,2048]{2,0,1:T(8,128)(2,1)}) %all-gather.8.cloned.1.call-update) | async-done | bytes 8388624 | tf_op jit(solution)/shard_map/all_gather | solution.py:202
  321.9 7.6 fusion.10
  329.5 13.1 %convert_reduce_fusion = (f32[512]{0:T(512)}, bf16[2048,512]{1,0:T(8,128)(2,1)S(1)}) fusion(f32[2048,512]{1,0:T(8,128)S(1)} %fusion.10, f32[512]{0:T(512)S(1)} %copy-done.98, bf16[512,2048]{1,0:T(8,128)(2,1)S(1)} %copy-done, bf16[2048,1,2048]{2,0,1:T(8,128)(2,1)} %all-gather.6.cloned.1.call-done), kind=kOutput, calls=%fused_computation.30 | convolution fusion | flops 4319084032 | bytes 16781312 | tf_op jit(solution)/shard_map/rsd,fd->rsf/dot_general | solution.py:217
  343.9 7.0 convert_bitcast_fusion.1
  351.4 84.2 %reduce-scatter.7.cloned.1.call-done = bf16[128,1,2048]{2,0,1:T(8,128)(2,1)} async-done(((bf16[2048,1,2048]{2,0,1:T(8,128)(2,1)}), bf16[128,1,2048]{2,0,1:T(8,128)(2,1)}) %reduce-scatter.7.cloned.1.call-update) | async-done | bytes 524304 | tf_op jit(solution)/shard_map/reduce_scatter | solution.py:231
  442.1 14.3 %collective-permute-done = bf16[128,1,2048]{2,0,1:T(8,128)(2,1)S(1)} collective-permute-done((bf16[128,1,2048]{2,0,1:T(8,128)(2,1)S(1)}, bf16[128,1,2048]{2,0,1:T(8,128)(2,1)S(1)}, u32[]{:S(2)}, u32[]{:S(2)}) %collective-permute-start) | collective-permute-done | bytes 524320 | tf_op jit(solution)/shard_map/ppermute | solution.py:25
  461.8 9.4 %collective-permute-done.1 = bf16[128,1,2048]{2,0,1:T(8,128)(2,1)S(1)} collective-permute-done((bf16[128,1,2048]{2,0,1:T(8,128)(2,1)S(1)}, bf16[128,1,2048]{2,0,1:T(8,128)(2,1)S(1)}, u32[]{:S(2)}, u32[]{:S(2)}) %collective-permute-start.1) | collective-permute-done | bytes 524320 | tf_op jit(solution)/shard_map/ppermute | solution.py:25
  476.6 8.6 %collective-permute-done.2 = bf16[128,1,2048]{2,0,1:T(8,128)(2,1)} collective-permute-done((bf16[128,1,2048]{2,0,1:T(8,128)(2,1)S(1)}, bf16[128,1,2048]{2,0,1:T(8,128)(2,1)}, u32[]{:S(2)}, u32[]{:S(2)}) %collective-permute-start.2) | collective-permute-done | bytes 524320 | tf_op jit(solution)/shard_map/ppermute | solution.py:25
  485.3 5.4 collective-permute-start.10
  490.7 7.8 collective-permute-done.3
  502.3 5.4 collective-permute-start.11
  515.2 5.8 collective-permute-start.12
  529.1 5.9 collective-permute-start.13
  540.1 7.2 convert_bitcast_fusion.2
  547.3 5.6 collective-permute-start.14
  577.1 8.3 gather_fusion
  585.4 5.9 fusion.45
  600.4 10.1 %multiply_reduce_fusion = (f32[512]{0:T(512)}, f32[512]{0:T(512)}, f32[512]{0:T(512)}, f32[512]{0:T(512)}, f32[512,2048]{1,0:T(8,128)}) fusion(f32[512,2048]{1,0:T(8,128)S(1)} %copy-done.4, f32[512]{0:T(512)S(1)} %copy-done.71, pred[2048]{0:T(1024)(128)(4,1)S(1)} %iota_compare_fusion.4, s32[512]{0:T(512)S(1)} %iota_add_fusion, f32[512,2048]{1,0:T(8,128)} %fusion.108, ...), kind=kOutput, calls=%fused_computation.32 | convolution fusion | flops 293599232 | bytes 34234368 | tf_op jit(solution)/shard_map/while/body/eval_jaxpr/dot_general | solution.py:87
  610.4 9.1 %multiply_convert_fusion = (bf16[512,2048]{1,0:T(8,128)(2,1)S(1)}, bf16[512,2048]{1,0:T(8,128)(2,1)}, bf16[512,2048]{1,0:T(8,128)(2,1)S(1)}) fusion(f32[512,2048]{1,0:T(8,128)} %get-tuple-element.119, f32[512]{0:T(512)} %get-tuple-element.82, f32[512,2048]{1,0:T(8,128)S(1)} %copy-done.4, f32[512]{0:T(512)} %get-tuple-element.124, ...), kind=kLoop, calls=%fused_computation.31 | loop fusion | flops 22020096 | bytes 31475712 | tf_op jit(solution)/shard_map/while/body/eval_jaxpr/convert_element_type | solution.py:91
  638.8 9.7 %convert_bitcast_fusion = bf16[2048,1,2048]{2,0,1:T(8,128)(2,1)} fusion(bf16[2048,384]{0,1:T(8,128)(2,1)} %bitcast.239, bf16[2048,384]{0,1:T(8,128)(2,1)} %bitcast.240), kind=kOutput, calls=%fused_computation.17 | convolution fusion | flops 3225419776 | bytes 11534336 | tf_op jit(solution)/shard_map/rsc,dc->rsd/dot_general | solution.py:272
  651.9 8.9 %fusion.27 = f32[512,2048]{1,0:T(8,128)S(1)} fusion(bf16[2048,1,2048]{2,0,1:T(8,128)(2,1)} %all-gather.6.cloned.1.call-done, f32[]{:T(128)S(6)} %div.167, f32[2048,512]{1,0:T(8,128)} %copy-done.100, f32[512]{0:T(512)S(1)} %copy-done.99), kind=kOutput, calls=%fused_computation.60 | convolution fusion | flops 4306501632 | bytes 16779268 | tf_op jit(solution)/shard_map/rsf,rsd->fd/dot_general | solution.py:216
  672.6 7.2 fusion.30
  686.7 10.6 %collective-permute-done.31 = bf16[512,4,256]{2,0,1:T(8,128)(2,1)} collective-permute-done((bf16[512,4,256]{2,0,1:T(8,128)(2,1)}, bf16[512,4,256]{2,0,1:T(8,128)(2,1)}, u32[]{:S(2)}, u32[]{:S(2)}) %collective-permute-start.31) | collective-permute-done | bytes 1048608 | tf_op jit(solution)/shard_map/ppermute | solution.py:364
  699.5 9.2 %collective-permute-done.28 = bf16[4,256,512]{2,1,0:T(8,128)(2,1)} collective-permute-done((bf16[4,256,512]{2,1,0:T(8,128)(2,1)}, bf16[4,256,512]{2,1,0:T(8,128)(2,1)}, u32[]{:S(2)}, u32[]{:S(2)}) %collective-permute-start.28) | collective-permute-done | bytes 1048608 | tf_op jit(solution)/shard_map/ppermute | solution.py:364
  739.2 7.0 fusion.36
  762.4 29.7 %collective-permute-done.22 = bf16[4,256,3,1,128]{4,3,2,1,0:T(2,128)(2,1)} collective-permute-done((bf16[4,256,3,1,128]{4,3,2,1,0:T(2,128)(2,1)S(1)}, bf16[4,256,3,1,128]{4,3,2,1,0:T(2,128)(2,1)}, u32[]{:S(2)}, u32[]{:S(2)}) %collective-permute-start.22) | collective-permute-done | bytes 786464 | tf_op jit(solution)/shard_map/ppermute | solution.py:364
  810.1 5.7 collective-permute-done.24
  (441 shorter events, 250.9 us)
Async XLA Ops:
  7.2 78.3 %all-gather.4.cloned.1.call-start = ((), (), s32[]{:S(2)}) async-start(), calls=%async_computation.4 | async-start | bytes 8912896 | tf_op jit(solution)/shard_map/all_gather | solution.py:154
  12.2 146.3 %all-gather.6.cloned.1.call-start = ((), (), s32[]{:S(2)}) async-start(), calls=%async_computation.5 | async-start | bytes 8912896 | tf_op jit(solution)/shard_map/all_gather | solution.py:189
  16.8 229.8 %reduce-scatter.5.cloned.1.call-start = ((), (), s32[]{:S(2)}) async-start(), calls=%async_computation.6 | async-start | bytes 8912896 | tf_op jit(solution)/shard_map/reduce_scatter | solution.py:195
  158.6 163.3 %all-gather.8.cloned.1.call-start = ((), (), s32[]{:S(2)}) async-start(), calls=%async_computation.7 | async-start | bytes 8912896 | tf_op jit(solution)/shard_map/all_gather | solution.py:202
  251.6 183.9 %reduce-scatter.7.cloned.1.call-start = ((), (), s32[]{:S(2)}) async-start(), calls=%async_computation.8 | async-start | bytes 8912896 | tf_op jit(solution)/shard_map/reduce_scatter | solution.py:231
  351.0 406.9 %reduce-scatter.11.cloned.1.call-start = ((), (), s32[]{:S(2)}) async-start(), calls=%async_computation.10 | async-start | bytes 8912896 | tf_op jit(solution)/shard_map/reduce_scatter | solution.py:271
  440.6 15.8 %collective-permute-start = (bf16[128,1,2048]{2,0,1:T(8,128)(2,1)S(1)}, bf16[128,1,2048]{2,0,1:T(8,128)(2,1)S(1)}, u32[]{:S(2)}, u32[]{:S(2)}) collective-permute-start(bf16[128,1,2048]{2,0,1:T(8,128)(2,1)S(1)} %get-tuple-element.89), channel_id=1, source_target_pairs={{0,1},{1,2},{2,3},{3,4},{4,5},{5,6},{6,7},{7,8},{8,9},{9,10},{10,1... | collective-permute-start | bytes 1572872 | tf_op jit(solution)/shard_map/ppermute | solution.py:25
  456.4 14.8 %collective-permute-start.1 = (bf16[128,1,2048]{2,0,1:T(8,128)(2,1)S(1)}, bf16[128,1,2048]{2,0,1:T(8,128)(2,1)S(1)}, u32[]{:S(2)}, u32[]{:S(2)}) collective-permute-start(bf16[128,1,2048]{2,0,1:T(8,128)(2,1)S(1)} %collective-permute-done), channel_id=1, source_target_pairs={{0,1},{1,2},{2,3},{3,4},{4,5},{5,6},{6,7},{7,8},{8,9},{9,10},{10,1... | collective-permute-start | bytes 1572872 | tf_op jit(solution)/shard_map/ppermute | solution.py:25
  456.4 14.8 %collective-permute-start.8 = (bf16[128,1,2048]{2,0,1:T(8,128)(2,1)S(1)}, bf16[128,1,2048]{2,0,1:T(8,128)(2,1)}, u32[]{:S(2)}, u32[]{:S(2)}) collective-permute-start(bf16[128,1,2048]{2,0,1:T(8,128)(2,1)S(1)} %get-tuple-element.89), channel_id=1, source_target_pairs={{1,0},{2,1},{3,2},{4,3},{5,4},{6,5},{7,6},{8,7},{9,8},{10,9},{11,1... | collective-permute-start | bytes 1572872 | tf_op jit(solution)/shard_map/ppermute | solution.py:27
  471.2 14.0 %collective-permute-start.2 = (bf16[128,1,2048]{2,0,1:T(8,128)(2,1)S(1)}, bf16[128,1,2048]{2,0,1:T(8,128)(2,1)}, u32[]{:S(2)}, u32[]{:S(2)}) collective-permute-start(bf16[128,1,2048]{2,0,1:T(8,128)(2,1)S(1)} %collective-permute-done.1), channel_id=1, source_target_pairs={{0,1},{1,2},{2,3},{3,4},{4,5},{5,6},{6,7},{7,8},{8,9},{9,10},{10,1... | collective-permute-start | bytes 1572872 | tf_op jit(solution)/shard_map/ppermute | solution.py:25
  471.2 14.0 %collective-permute-start.9 = (bf16[128,1,2048]{2,0,1:T(8,128)(2,1)}, bf16[128,1,2048]{2,0,1:T(8,128)(2,1)}, u32[]{:S(2)}, u32[]{:S(2)}) collective-permute-start(bf16[128,1,2048]{2,0,1:T(8,128)(2,1)} %collective-permute-done.8), channel_id=1, source_target_pairs={{1,0},{2,1},{3,2},{4,3},{5,4},{6,5},{7,6},{8,7},{9,8},{10,9},{11,1... | collective-permute-start | bytes 1572872 | tf_op jit(solution)/shard_map/ppermute | solution.py:27
  485.2 13.3 %collective-permute-start.3 = (bf16[128,1,2048]{2,0,1:T(8,128)(2,1)}, bf16[128,1,2048]{2,0,1:T(8,128)(2,1)}, u32[]{:S(2)}, u32[]{:S(2)}) collective-permute-start(bf16[128,1,2048]{2,0,1:T(8,128)(2,1)} %collective-permute-done.2), channel_id=1, source_target_pairs={{0,1},{1,2},{2,3},{3,4},{4,5},{5,6},{6,7},{7,8},{8,9},{9,10},{10,1... | collective-permute-start | bytes 1572872 | tf_op jit(solution)/shard_map/ppermute | solution.py:25
  485.3 17.0 %collective-permute-start.10 = (bf16[128,1,2048]{2,0,1:T(8,128)(2,1)}, bf16[128,1,2048]{2,0,1:T(8,128)(2,1)S(1)}, u32[]{:S(2)}, u32[]{:S(2)}) collective-permute-start(bf16[128,1,2048]{2,0,1:T(8,128)(2,1)} %collective-permute-done.9), channel_id=1, source_target_pairs={{1,0},{2,1},{3,2},{4,3},{5,4},{6,5},{7,6},{8,7},{9,8},{10,9},{11,1... | collective-permute-start | bytes 1572872 | tf_op jit(solution)/shard_map/ppermute | solution.py:27
  498.5 13.0 %collective-permute-start.4 = (bf16[128,1,2048]{2,0,1:T(8,128)(2,1)}, bf16[128,1,2048]{2,0,1:T(8,128)(2,1)S(1)}, u32[]{:S(2)}, u32[]{:S(2)}) collective-permute-start(bf16[128,1,2048]{2,0,1:T(8,128)(2,1)} %collective-permute-done.3), channel_id=1, source_target_pairs={{0,1},{1,2},{2,3},{3,4},{4,5},{5,6},{6,7},{7,8},{8,9},{9,10},{10,1... | collective-permute-start | bytes 1572872 | tf_op jit(solution)/shard_map/ppermute | solution.py:25
  502.3 12.1 %collective-permute-start.11 = (bf16[128,1,2048]{2,0,1:T(8,128)(2,1)S(1)}, bf16[128,1,2048]{2,0,1:T(8,128)(2,1)S(1)}, u32[]{:S(2)}, u32[]{:S(2)}) collective-permute-start(bf16[128,1,2048]{2,0,1:T(8,128)(2,1)S(1)} %collective-permute-done.10), channel_id=1, source_target_pairs={{1,0},{2,1},{3,2},{4,3},{5,4},{6,5},{7,6},{8,7},{9,8},{10,9},{11,1... | collective-permute-start | bytes 1572872 | tf_op jit(solution)/shard_map/ppermute | solution.py:27
  511.5 13.9 %collective-permute-start.5 = (bf16[128,1,2048]{2,0,1:T(8,128)(2,1)S(1)}, bf16[128,1,2048]{2,0,1:T(8,128)(2,1)S(1)}, u32[]{:S(2)}, u32[]{:S(2)}) collective-permute-start(bf16[128,1,2048]{2,0,1:T(8,128)(2,1)S(1)} %collective-permute-done.4), channel_id=1, source_target_pairs={{0,1},{1,2},{2,3},{3,4},{4,5},{5,6},{6,7},{7,8},{8,9},{9,10},{10,1... | collective-permute-start | bytes 1572872 | tf_op jit(solution)/shard_map/ppermute | solution.py:25
  515.2 13.9 %collective-permute-start.12 = (bf16[128,1,2048]{2,0,1:T(8,128)(2,1)S(1)}, bf16[128,1,2048]{2,0,1:T(8,128)(2,1)}, u32[]{:S(2)}, u32[]{:S(2)}) collective-permute-start(bf16[128,1,2048]{2,0,1:T(8,128)(2,1)S(1)} %collective-permute-done.11), channel_id=1, source_target_pairs={{1,0},{2,1},{3,2},{4,3},{5,4},{6,5},{7,6},{8,7},{9,8},{10,9},{11,1... | collective-permute-start | bytes 1572872 | tf_op jit(solution)/shard_map/ppermute | solution.py:27
  525.3 14.7 %collective-permute-start.6 = (bf16[128,1,2048]{2,0,1:T(8,128)(2,1)S(1)}, bf16[128,1,2048]{2,0,1:T(8,128)(2,1)}, u32[]{:S(2)}, u32[]{:S(2)}) collective-permute-start(bf16[128,1,2048]{2,0,1:T(8,128)(2,1)S(1)} %collective-permute-done.5), channel_id=1, source_target_pairs={{0,1},{1,2},{2,3},{3,4},{4,5},{5,6},{6,7},{7,8},{8,9},{9,10},{10,1... | collective-permute-start | bytes 1572872 | tf_op jit(solution)/shard_map/ppermute | solution.py:25
  529.1 18.2 %collective-permute-start.13 = (bf16[128,1,2048]{2,0,1:T(8,128)(2,1)}, bf16[128,1,2048]{2,0,1:T(8,128)(2,1)}, u32[]{:S(2)}, u32[]{:S(2)}) collective-permute-start(bf16[128,1,2048]{2,0,1:T(8,128)(2,1)} %collective-permute-done.12), channel_id=1, source_target_pairs={{1,0},{2,1},{3,2},{4,3},{5,4},{6,5},{7,6},{8,7},{9,8},{10,9},{11,1... | collective-permute-start | bytes 1572872 | tf_op jit(solution)/shard_map/ppermute | solution.py:27
  540.1 12.8 %collective-permute-start.7 = (bf16[128,1,2048]{2,0,1:T(8,128)(2,1)}, bf16[128,1,2048]{2,0,1:T(8,128)(2,1)}, u32[]{:S(2)}, u32[]{:S(2)}) collective-permute-start(bf16[128,1,2048]{2,0,1:T(8,128)(2,1)} %collective-permute-done.6), channel_id=1, source_target_pairs={{0,1},{1,2},{2,3},{3,4},{4,5},{5,6},{6,7},{7,8},{8,9},{9,10},{10,1... | collective-permute-start | bytes 1572872 | tf_op jit(solution)/shard_map/ppermute | solution.py:25
  547.3 28.9 %collective-permute-start.14 = (bf16[128,1,2048]{2,0,1:T(8,128)(2,1)}, bf16[128,1,2048]{2,0,1:T(8,128)(2,1)S(1)}, u32[]{:S(2)}, u32[]{:S(2)}) collective-permute-start(bf16[128,1,2048]{2,0,1:T(8,128)(2,1)} %collective-permute-done.13), channel_id=1, source_target_pairs={{1,0},{2,1},{3,2},{4,3},{5,4},{6,5},{7,6},{8,7},{9,8},{10,9},{11,1... | collective-permute-start | bytes 1572872 | tf_op jit(solution)/shard_map/ppermute | solution.py:27
  648.5 170.8 %reduce-scatter.9.cloned.1.call-start = ((), (), s32[]{:S(2)}) async-start(), calls=%async_computation.9 | async-start | bytes 8912896 | tf_op jit(solution)/shard_map/reduce_scatter | solution.py:248
  670.9 26.4 %collective-permute-start.31 = (bf16[512,4,256]{2,0,1:T(8,128)(2,1)}, bf16[512,4,256]{2,0,1:T(8,128)(2,1)}, u32[]{:S(2)}, u32[]{:S(2)}) collective-permute-start(bf16[512,4,256]{2,0,1:T(8,128)(2,1)} %select_convert_fusion), channel_id=1, source_target_pairs={{0,64},{32,96},{64,0},{96,32},{1,65},{33,97},{65,1},{97,33},{2,66}... | collective-permute-start | bytes 3145736 | tf_op jit(solution)/shard_map/ppermute | solution.py:364
  682.2 26.6 %collective-permute-start.28 = (bf16[4,256,512]{2,1,0:T(8,128)(2,1)}, bf16[4,256,512]{2,1,0:T(8,128)(2,1)}, u32[]{:S(2)}, u32[]{:S(2)}) collective-permute-start(bf16[4,256,512]{2,1,0:T(8,128)(2,1)} %bitcast.76), channel_id=1, source_target_pairs={{0,64},{32,96},{64,0},{96,32},{1,65},{33,97},{65,1},{97,33},{2,66}... | collective-permute-start | bytes 3145736 | tf_op jit(solution)/shard_map/ppermute | solution.py:364
  699.4 11.2 %collective-permute-start.32 = (bf16[512,2,256]{2,0,1:T(8,128)(2,1)S(1)}, bf16[512,2,256]{2,0,1:T(8,128)(2,1)S(1)}, u32[]{:S(2)}, u32[]{:S(2)}) collective-permute-start(bf16[512,2,256]{2,0,1:T(8,128)(2,1)S(1)} %select_convert_fusion.3), channel_id=1, source_target_pairs={{0,32},{32,0},{64,96},{96,64},{1,33},{33,1},{65,97},{97,65},{2,34}... | collective-permute-start | bytes 1572872 | tf_op jit(solution)/shard_map/ppermute | solution.py:364
  711.6 11.0 %collective-permute-start.33 = (bf16[512,1,256]{2,0,1:T(8,128)(2,1)}, bf16[512,1,256]{2,0,1:T(8,128)(2,1)S(1)}, u32[]{:S(2)}, u32[]{:S(2)}) collective-permute-start(bf16[512,1,256]{2,0,1:T(8,128)(2,1)} %select_convert_fusion.5), channel_id=1, source_target_pairs={{0,16},{16,0},{1,17},{17,1},{2,18},{18,2},{3,19},{19,3},{4,20},{20... | collective-permute-start | bytes 786440 | tf_op jit(solution)/shard_map/ppermute | solution.py:364
  716.5 11.4 %collective-permute-start.30 = (bf16[1,256,512]{2,1,0:T(8,128)(2,1)S(1)}, bf16[1,256,512]{2,1,0:T(8,128)(2,1)S(1)}, u32[]{:S(2)}, u32[]{:S(2)}) collective-permute-start(bf16[1,256,512]{2,1,0:T(8,128)(2,1)S(1)} %select_convert_fusion.6), channel_id=1, source_target_pairs={{0,16},{16,0},{1,17},{17,1},{2,18},{18,2},{3,19},{19,3},{4,20},{20... | collective-permute-start | bytes 786440 | tf_op jit(solution)/shard_map/ppermute | solution.py:364
  737.6 10.1 %collective-permute-start.25 = (bf16[1,128,4,256]{3,1,2,0:T(8,128)(2,1)S(1)}, bf16[1,128,4,256]{3,1,2,0:T(8,128)(2,1)S(1)}, u32[]{:S(2)}, u32[]{:S(2)}) collective-permute-start(bf16[1,128,4,256]{3,1,2,0:T(8,128)(2,1)S(1)} %select_convert_fusion.7), channel_id=1, source_target_pairs={{0,64},{32,96},{64,0},{96,32},{1,65},{33,97},{65,1},{97,33},{2,66}... | collective-permute-start | bytes 786440 | tf_op jit(solution)/shard_map/ppermute | solution.py:364
  755.7 36.4 %collective-permute-start.22 = (bf16[4,256,3,1,128]{4,3,2,1,0:T(2,128)(2,1)S(1)}, bf16[4,256,3,1,128]{4,3,2,1,0:T(2,128)(2,1)}, u32[]{:S(2)}, u32[]{:S(2)}) collective-permute-start(bf16[4,256,3,1,128]{4,3,2,1,0:T(2,128)(2,1)S(1)} %copy.55), channel_id=1, source_target_pairs={{0,64},{32,96},{64,0},{96,32},{1,65},{33,97},{65,1},{97,33},{2,66}... | collective-permute-start | bytes 2359304 | tf_op jit(solution)/shard_map/ppermute | solution.py:364
  762.3 34.1 %collective-permute-start.15 = (f32[8,8,192]{2,0,1:T(8,128)S(1)}, f32[8,8,192]{2,0,1:T(8,128)S(1)}, u32[]{:S(2)}, u32[]{:S(2)}) collective-permute-start(f32[8,8,192]{2,0,1:T(8,128)S(1)} %slice_select_fusion.2), channel_id=1, source_target_pairs={{0,8},{1,9},{2,10},{3,11},{4,12},{5,13},{6,14},{7,15},{8,0},{9,1},... | collective-permute-start | bytes 147464 | tf_op jit(solution)/shard_map/ppermute | solution.py:364
  806.4 9.4 %collective-permute-start.24 = (bf16[1,256,3,1,128]{4,3,2,1,0:T(2,128)(2,1)S(1)}, bf16[1,256,3,1,128]{4,3,2,1,0:T(2,128)(2,1)S(1)}, u32[]{:S(2)}, u32[]{:S(2)}) collective-permute-start(bf16[1,256,3,1,128]{4,3,2,1,0:T(2,128)(2,1)S(1)} %fusion.96), channel_id=1, source_target_pairs={{0,16},{16,0},{1,17},{17,1},{2,18},{18,2},{3,19},{19,3},{4,20},{20... | collective-permute-start | bytes 589832 | tf_op jit(solution)/shard_map/ppermute | solution.py:364
  809.7 7.5 collective-permute-start.19
  (113 other events, 2519.4 us)
Sparse Core Ops, SparseCore 0:
  12.4 73.0 all-gather.3
  88.2 70.3 all-gather.5
  162.0 84.6 reduce-scatter.4
  251.8 70.0 all-gather.7
  351.1 84.4 reduce-scatter.6
  648.7 81.5 reduce-scatter.10
  733.6 84.6 reduce-scatter.8
